TPU v7x, 32 devices: a whole 2x2x4 slice. The times are simulated.
32 devices in a mesh: dec: 2 (over x), ada: 16 (over z, y, core).
Axes of the slice: x: 2, y: 2, z: 4, core: 2. Of those that a mesh axis runs over, the one named last changes fastest.
Arguments:
- inputs: bfloat16 [4, 64, 8192], P(None, ('dec', 'ada')), may hold values from -6 to 6
- query_weight: bfloat16 [8192, 8192], P(None, 'ada'), may hold values from -0.0625 to 0.0625
- adapter_down: bfloat16 [32, 8192, 64], P(('dec', 'ada')), may hold values from -0.0625 to 0.0625
- adapter_up: bfloat16 [32, 64, 8192], P(('dec', 'ada')), may hold values from -0.75 to 0.75
- adapter_ids: int32 [64, 1], P(('dec', 'ada')), may hold values from 0 to 15; in each aligned block of 32 rows (0 to 31, 32 to 63, ...) at most 4 rows name the same one
- new_cache: bfloat16 [4, 64, 2, 1024], P(None, ('dec', 'ada')), may hold values from -9 to 9
- cache_pool: bfloat16 [256, 2, 16, 1024], P(('dec', 'ada')), may hold values from -400 to 400
- page_table: int32 [64, 4], P(('dec', 'ada')), may hold values from 0 to 15, as said below
- lengths: int32 [64], P(('dec', 'ada')), may hold values from 1 to 64, as said below
Outputs:
- attended: bfloat16 [4, 64, 8192], P(None, ('dec', 'ada'))
Inputs may be any that keep to these rules, and one draw needn't show every extreme that they name: `adapter_ids`: in each aligned block of 32 rows (one decode group) no id is named by more than 4 rows, a bound that some block reaches. `page_table`: entries j >= ceil(lengths[r] / 16) are unused. Among rows with the same (r % 32) // 2, the live entries are all different. `lengths`: among rows with the same (r % 32) // 2, one reaches 64.
All inputs are finite; a program needn't handle non-finite values.
Results may differ from a plain program's by a relative error of at most 0.007.
The roundings to bfloat16 on the way count: a program that leaves them out, or rounds other values in their place, can miss the bound.
Values may be sent and summed in bfloat16 or wider, within the bound.
A program may use at most 64 MiB of HBM per device.

v0:
```python
import math

import jax
import jax.numpy as jnp
from jax import lax
from jax.sharding import PartitionSpec as P

HEADS = 64
KVH = 8
HD = 128
CAP = 4


NEGATIVE = -1e30
HIGH = lax.Precision.HIGHEST


def cache_part(query, keys, values, live):
    scale = 1.0 / math.sqrt(query.shape[-1])
    scores = (
        jnp.einsum("trkgd,rpkd->trkgp", query, keys, preferred_element_type=jnp.float32) * scale
    )
    mask = live[None, :, None, None, :]
    scores = jnp.where(mask, scores, NEGATIVE)
    top = jnp.max(scores, axis=-1)
    weights = jnp.where(mask, jnp.exp(scores - top[..., None]), 0.0)
    numerator = jnp.einsum("trkgp,rpkd->trkgd", weights, values.astype(jnp.float32), precision=HIGH)
    return (numerator, top, jnp.sum(weights, axis=-1))


def fresh_part(query, new_entries):
    steps, rows, kv_heads, group, head_dim = query.shape
    scale = 1.0 / math.sqrt(head_dim)
    keys = new_entries[:, :, 0].reshape(new_entries.shape[0], rows, kv_heads, head_dim)
    values = new_entries[:, :, 1].reshape(new_entries.shape[0], rows, kv_heads, head_dim)
    scores = (
        jnp.einsum("trkgd,urkd->trkgu", query, keys, preferred_element_type=jnp.float32) * scale
    )
    allowed = (jnp.arange(new_entries.shape[0])[None, :] <= jnp.arange(steps)[:, None])[
        :, None, None, None, :
    ]
    scores = jnp.where(allowed, scores, NEGATIVE)
    top = jnp.max(scores, axis=-1)
    weights = jnp.where(allowed, jnp.exp(scores - top[..., None]), 0.0)
    numerator = jnp.einsum("trkgu,urkd->trkgd", weights, values.astype(jnp.float32), precision=HIGH)
    return (numerator, top, jnp.sum(weights, axis=-1))


def body(
    inputs,
    query_weight,
    adapter_down,
    adapter_up,
    adapter_ids,
    new_cache,
    cache_pool,
    page_table,
    lengths,
):
    steps, row_local, width = inputs.shape
    adapter_total_count = lax.axis_size("ada")
    dec_count = lax.axis_size("dec")
    head_cols = query_weight.shape[1]
    held_adapters = adapter_down.shape[0]
    adapter_rank = adapter_down.shape[2]
    group = row_local * adapter_total_count
    capacity = CAP
    slots = held_adapters * capacity
    whole_inputs, group_ids = (
        lax.all_gather(inputs, "ada", axis=1, tiled=True),
        lax.all_gather(adapter_ids, "ada", axis=0, tiled=True),
    )
    base_output = jnp.dot(
        whole_inputs.reshape(steps * group, width), query_weight, preferred_element_type=jnp.float32
    )
    base_output = base_output.reshape(steps, group, head_cols)
    row_adapter = group_ids[:, 0]
    order = jnp.arange(group)
    earlier = (row_adapter[:, None] == row_adapter[None, :]) & (order[None, :] < order[:, None])
    earlier_count = jnp.sum(earlier.astype(jnp.int32), axis=1)
    slot_of_row = (
        row_adapter // held_adapters * slots
        + row_adapter % held_adapters * capacity
        + earlier_count
    )
    local_slot = slot_of_row - lax.axis_index("ada") * slots
    pick = (local_slot[None, :] == jnp.arange(slots)[:, None]).astype(jnp.bfloat16)
    chosen = jnp.einsum(
        "sg,tgd->tsd", pick, whole_inputs, preferred_element_type=jnp.float32
    ).astype(jnp.bfloat16)
    chosen = chosen.reshape(steps, held_adapters, capacity, width)
    shrink = jnp.einsum(
        "tjcd,jdr->tjcr", chosen, adapter_down, preferred_element_type=jnp.float32
    ).astype(jnp.bfloat16)
    columns = lax.all_to_all(adapter_up, "ada", split_axis=2, concat_axis=0, tiled=True)
    every_shrink = lax.all_gather(
        shrink.reshape(steps, slots, adapter_rank), "ada", axis=1, tiled=True
    )
    every_shrink = every_shrink.reshape(
        steps, adapter_total_count * held_adapters, capacity, adapter_rank
    )
    received_rows = jnp.einsum(
        "tacr,arh->tach", every_shrink, columns, preferred_element_type=jnp.float32
    ).astype(jnp.bfloat16)
    received_rows = received_rows.reshape(steps, adapter_total_count * slots, head_cols)
    slot_position = (
        slot_of_row[:, None] == jnp.arange(adapter_total_count * slots)[None, :]
    ).astype(jnp.bfloat16)
    low_rank_update = jnp.einsum(
        "mr,urx->umx", slot_position, received_rows, preferred_element_type=jnp.float32
    )
    query_columns = (base_output + low_rank_update).astype(jnp.bfloat16)
    query_local = lax.all_to_all(query_columns, "ada", split_axis=1, concat_axis=2, tiled=True)
    group_heads = HEADS // KVH
    query = query_local.reshape(steps, row_local, KVH, group_heads, HD)
    fresh = fresh_part(query, new_cache)
    pool_local = cache_pool.shape[0]
    page_length = cache_pool.shape[2]
    table_width = page_table.shape[1]
    position = jnp.arange(table_width * page_length)
    every_query, every_table, every_length = (
        lax.all_gather(query_local, "dec", axis=1, tiled=True),
        lax.all_gather(page_table, "dec", axis=0, tiled=True),
        lax.all_gather(lengths, "dec", axis=0, tiled=True),
    )
    column_rows = dec_count * row_local
    asked = every_query.reshape(steps, column_rows, KVH, group_heads, HD)
    local = every_table // pool_local == lax.axis_index("dec")
    pages = cache_pool[every_table % pool_local]
    keys = pages[:, :, 0].reshape(column_rows, table_width * page_length, KVH, HD)
    values = pages[:, :, 1].reshape(column_rows, table_width * page_length, KVH, HD)
    live = (position[None, :] < every_length[:, None]) & jnp.repeat(local, page_length, axis=1)
    partial_numerator, part_top, part_total = cache_part(asked, keys, values, live)
    partial_numerator = partial_numerator.reshape(steps, dec_count, row_local, KVH, group_heads, HD)
    part_top = part_top.reshape(steps, dec_count, row_local, KVH, group_heads)
    part_total = part_total.reshape(steps, dec_count, row_local, KVH, group_heads)
    back_numerator, back_top, back_total = (
        lax.all_to_all(partial_numerator, "dec", split_axis=1, concat_axis=1, tiled=True),
        lax.all_to_all(part_top, "dec", split_axis=1, concat_axis=1, tiled=True),
        lax.all_to_all(part_total, "dec", split_axis=1, concat_axis=1, tiled=True),
    )
    top = jnp.maximum(jnp.max(back_top, axis=1), fresh[1])
    factor = jnp.exp(back_top - top[:, None])
    numerator = (
        jnp.sum(back_numerator * factor[..., None], axis=1)
        + fresh[0] * jnp.exp(fresh[1] - top)[..., None]
    )
    total = jnp.sum(back_total * factor, axis=1) + fresh[2] * jnp.exp(fresh[1] - top)
    attended = (numerator / total[..., None]).astype(jnp.bfloat16)
    return attended.reshape(steps, row_local, width)


def solution(mesh):
    in_specs = (
        P(None, ("dec", "ada"), None),
        P(None, "ada"),
        P(("dec", "ada"), None, None),
        P(("dec", "ada"), None, None),
        P(("dec", "ada"), None),
        P(None, ("dec", "ada"), None, None),
        P(("dec", "ada"), None, None, None),
        P(("dec", "ada"), None),
        P(("dec", "ada")),
    )
    out_specs = P(None, ("dec", "ada"), None)
    return jax.shard_map(body, mesh=mesh, in_specs=in_specs, out_specs=out_specs, check_vma=False)
```

profile of v0, /device:TPU:0, one launch (start us, length us, event | category | flops | bytes accessed | tf_op | source)
XLA Modules:
  0.0 197.2 jit_solution(16430546696477317186)
XLA Ops:
  6.5 1.8 copy.73
  8.3 9.2 %copy.78 = bf16[1,64,8192]{1,0,2:T(2,128)(2,1)} copy(bf16[1,64,8192]{2,1,0:T(8,128)(2,1)} %param.12) | data formatting | bytes 2097152 | tf_op args[3]
  17.5 0.5 broadcast.160
  18.0 45.2 %reduce.4 = bf16[8192,64]{1,0:T(8,128)(2,1)S(1)} reduce(bf16[8192,1,64]{2,1,0:T(2,128)(2,1)} %bitcast.122, bf16[]{:T(256)} %broadcast.160), dimensions={1}, to_apply=%bitcast.103.reduce_sub_computation | reduce | bytes 2097154
  63.2 2.3 %reshape.164 = bf16[16,2,16384]{2,1,0:T(2,128)(2,1)} reshape(bf16[8192,64]{1,0:T(8,128)(2,1)S(1)} %reduce.4) | data formatting | bytes 2097152
  65.5 7.4 %all-to-all-start = ((bf16[16,2,16384]{2,1,0:T(2,128)(2,1)}), bf16[16,2,16384]{2,1,0:T(2,128)(2,1)S(1)}, u32[]{:S(2)}, u32[]{:S(2)}) async-start(bf16[16,2,16384]{2,1,0:T(2,128)(2,1)} %reshape.164), calls=%async_computation | async-start | bytes 2097152 | tf_op jit(solution)/shard_map/all_to_all | solution.py:95
  72.9 4.2 %all-gather = s32[2,2,4]{2,1,0:T(2,128)S(1)} all-gather(s32[1,2,4]{2,1,0:T(2,128)S(1)} %bitcast.148), channel_id=1, replica_groups=mesh['dec'=2,'ada'=16] {'dec'}, dimensions={0}, use_global_device_ids=true | all-gather | bytes 96 | tf_op jit(solution)/shard_map/all_gather | solution.py:123
  77.2 0.7 dynamic-slice
  78.6 0.2 dynamic-update-slice
  78.8 4.3 %all-reduce = s32[4]{0:T(128)S(1)} all-reduce(s32[4]{0:T(128)S(1)} %dynamic-update-slice), channel_id=1, replica_groups=mesh['dec'=2,'ada'=16] {'dec'}, use_global_device_ids=true, to_apply=%add | all-reduce | flops 4 | bytes 32
  83.1 0.7 dynamic-slice.1
  84.9 1.7 gather_fusion
  86.8 0.9 copy.118
  87.8 12.3 %all-reduce.1 = s32[32]{0:T(128)S(1)} all-reduce(s32[32]{0:T(128)S(1)} %bitcast_dynamic-update-slice_fusion), channel_id=1, replica_groups=mesh['dec'=2,'ada'=16] {'ada'}, use_global_device_ids=true, to_apply=%add.1 | all-reduce | flops 32 | bytes 256 | tf_op jit(solution)/shard_map/squeeze | solution.py:77
  100.2 0.2 convert_reduce_fusion
  100.4 0.9 bitcast_bitcast_fusion
  101.3 7.0 %reshape.165 = bf16[8192,1,64]{2,1,0:T(2,128)(2,1)} reshape(bf16[16,2,16384]{2,1,0:T(2,128)(2,1)S(1)} %all-to-all-done) | data formatting | bytes 2097152
  108.3 2.5 %copy.115 = bf16[1,64,8192]{1,2,0:T(8,128)(2,1)S(1)} copy(bf16[1,64,8192]{1,0,2:T(2,128)(2,1)} %bitcast.123) | data formatting | bytes 2097152
  110.8 1.6 copy.80
  112.4 4.4 %fusion.19 = bf16[4,4,64]{2,1,0:T(4,128)(2,1)S(1)} fusion(bf16[4,32,8192]{2,0,1:T(4,128)(2,1)} %all-gather.3.cloned.1.call-done, bf16[1,8192,64]{1,2,0:T(8,128)(2,1)S(1)} %copy-done, s32[32]{0:T(128)S(1)} %get-tuple-element.11), kind=kOutput, calls=%fused_computation.24 | convolution fusion | flops 25298048 | bytes 3147904 | tf_op jit(solution)/shard_map/tjcd,jdr->tjcr/dot_general | solution.py:92
  116.8 19.0 %all_gather.22 = bf16[4,64,64]{2,0,1:T(4,128)(2,1)S(1)} all-gather(bf16[4,4,64]{2,0,1:T(4,128)(2,1)S(1)} %copy.76), channel_id=1, replica_groups=mesh['dec'=2,'ada'=16] {'ada'}, dimensions={1}, use_global_device_ids=true | all-gather | bytes 34816 | tf_op jit(solution)/shard_map/all_gather | solution.py:96
  135.8 1.5 fusion.7
  137.4 5.7 %fusion.1 = f32[4,32,512]{2,1,0:T(8,128)S(1)} fusion(bf16[8192,512]{1,0:T(8,128)(2,1)} %param.10, bf16[4,32,8192]{2,0,1:T(4,128)(2,1)S(1)} %copy-done.1), kind=kOutput, calls=%fused_computation.3 | convolution fusion | flops 1073741824 | bytes 10747904 | tf_op jit(solution)/shard_map/dot_general | solution.py:73
  143.2 0.2 fusion.15
  143.4 0.8 copy.84
  144.1 3.5 %all-to-all-start.1 = ((bf16[4,32,512]{2,0,1:T(4,128)(2,1)}), bf16[4,32,512]{2,0,1:T(4,128)(2,1)S(1)}, u32[]{:S(2)}, u32[]{:S(2)}) async-start(bf16[4,32,512]{2,0,1:T(4,128)(2,1)} %copy.84), calls=%async_computation.1 | async-start | bytes 262144 | tf_op jit(solution)/shard_map/all_to_all | solution.py:113
  147.7 1.1 bitcast_bitcast_fusion.1
  148.8 6.8 %all-to-all-done.1 = bf16[4,32,512]{2,0,1:T(4,128)(2,1)S(1)} async-done(((bf16[4,32,512]{2,0,1:T(4,128)(2,1)}), bf16[4,32,512]{2,0,1:T(4,128)(2,1)S(1)}, u32[]{:S(2)}, u32[]{:S(2)}) %all-to-all-start.1) | async-done | bytes 131104 | tf_op jit(solution)/shard_map/all_to_all | solution.py:113
  155.8 5.6 %all_gather.23 = bf16[4,4,8192]{2,0,1:T(4,128)(2,1)S(1)} all-gather(bf16[4,2,8192]{2,0,1:T(4,128)(2,1)S(1)} %all_to_all.42), channel_id=1, replica_groups=mesh['dec'=2,'ada'=16] {'dec'}, dimensions={1}, use_global_device_ids=true | all-gather | bytes 393216 | tf_op jit(solution)/shard_map/all_gather | solution.py:122
  161.4 0.3 reshape.161
  161.7 0.5 fusion.56
  162.2 0.4 fusion.27
  162.7 1.5 fusion.25
  164.1 0.7 reshape.166
  164.9 3.2 %all-to-all-start.3 = ((f32[2,1,512]{2,1,0:T(1,128)}), f32[2,1,512]{2,1,0:T(1,128)S(1)}, u32[]{:S(2)}, u32[]{:S(2)}) async-start(f32[2,1,512]{2,1,0:T(1,128)} %reshape.166), calls=%async_computation.3 | async-start | bytes 8192 | tf_op jit(solution)/shard_map/all_to_all | solution.py:139
  168.1 0.7 fusion.57
  169.0 0.7 reshape.168
  169.7 2.2 %all-to-all-done.3 = f32[2,1,512]{2,1,0:T(1,128)S(1)} async-done(((f32[2,1,512]{2,1,0:T(1,128)}), f32[2,1,512]{2,1,0:T(1,128)S(1)}, u32[]{:S(2)}, u32[]{:S(2)}) %all-to-all-start.3) | async-done | bytes 4128 | tf_op jit(solution)/shard_map/all_to_all | solution.py:139
  171.9 3.2 %all-to-all-start.4 = ((f32[2,1,512]{2,1,0:T(1,128)}), f32[2,1,512]{2,1,0:T(1,128)S(1)}, u32[]{:S(2)}, u32[]{:S(2)}) async-start(f32[2,1,512]{2,1,0:T(1,128)} %reshape.168), calls=%async_computation.4 | async-start | bytes 8192 | tf_op jit(solution)/shard_map/all_to_all | solution.py:140
  175.1 0.5 broadcast.161
  175.6 0.7 reduce.5
  176.4 2.4 %all-to-all-done.4 = f32[2,1,512]{2,1,0:T(1,128)S(1)} async-done(((f32[2,1,512]{2,1,0:T(1,128)}), f32[2,1,512]{2,1,0:T(1,128)S(1)}, u32[]{:S(2)}, u32[]{:S(2)}) %all-to-all-start.4) | async-done | bytes 4128 | tf_op jit(solution)/shard_map/all_to_all | solution.py:140
  178.9 3.5 %all-to-all-start.2 = ((f32[4,2,2,8,8,128]{5,4,0,3,2,1:T(8,128)}), f32[4,2,2,8,8,128]{5,4,0,3,2,1:T(8,128)S(1)}, u32[]{:S(2)}, u32[]{:S(2)}) async-start(f32[4,2,2,8,8,128]{5,4,0,3,2,1:T(8,128)} %bitcast.27), calls=%async_computation.2 | async-start | bytes 1048576 | tf_op jit(solution)/shard_map/all_to_all | solution.py:138
  182.4 0.7 reduce.6
  183.2 5.7 %all-to-all-done.2 = f32[4,2,2,8,8,128]{5,4,0,3,2,1:T(8,128)S(1)} async-done(((f32[4,2,2,8,8,128]{5,4,0,3,2,1:T(8,128)}), f32[4,2,2,8,8,128]{5,4,0,3,2,1:T(8,128)S(1)}, u32[]{:S(2)}, u32[]{:S(2)}) %all-to-all-start.2) | async-done | bytes 524320 | tf_op jit(solution)/shard_map/all_to_all | solution.py:138
  188.9 0.2 multiply_reduce_fusion
  189.1 0.5 fusion.16
  189.7 0.7 reshape.123
  (53 shorter events, 1.8 us)
Async XLA Ops:
  6.5 105.9 %copy-start = (bf16[1,8192,64]{1,2,0:T(8,128)(2,1)S(1)}, bf16[1,8192,64]{1,2,0:T(8,128)(2,1)}, u32[]{:S(2)}) copy-start(bf16[1,8192,64]{1,2,0:T(8,128)(2,1)} %param.11) | copy-start | bytes 3145732
  6.5 105.9 %all-gather.3.cloned.1.call-start = ((), (), s32[]{:S(2)}) async-start(), calls=%async_computation.5 | async-start | bytes 2228224 | tf_op jit(solution)/shard_map/all_gather | solution.py:70
  63.2 9.8 %copy-start.4 = (s32[2,4]{1,0:T(2,128)S(1)}, s32[2,4]{1,0:T(2,128)}, u32[]{:S(2)}) copy-start(s32[2,4]{1,0:T(2,128)} %param.16) | copy-start | bytes 100
  63.2 14.0 %copy-start.8 = (u32[32]{0:T(128)S(1)}, u32[32]{0:T(128)}, u32[]{:S(2)}) copy-start(u32[32]{0:T(128)} %constant.88) | copy-start | bytes 388
  63.2 15.4 %copy-start.5 = (s32[2]{0:T(128)S(1)}, s32[2]{0:T(128)}, u32[]{:S(2)}) copy-start(s32[2]{0:T(128)} %param.17) | copy-start | bytes 28
  63.2 19.9 %copy-start.7 = (u32[32]{0:T(128)S(1)}, u32[32]{0:T(128)}, u32[]{:S(2)}) copy-start(u32[32]{0:T(128)} %constant.93) | copy-start | bytes 388
  63.2 21.5 %copy-start.3 = (bf16[4,2,2,1024]{3,2,1,0:T(2,128)(2,1)S(1)}, bf16[4,2,2,1024]{3,2,1,0:T(2,128)(2,1)}, u32[]{:S(2)}) copy-start(bf16[4,2,2,1024]{3,2,1,0:T(2,128)(2,1)} %param.14) | copy-start | bytes 98308
  65.5 35.8 %all-to-all-start = ((bf16[16,2,16384]{2,1,0:T(2,128)(2,1)}), bf16[16,2,16384]{2,1,0:T(2,128)(2,1)S(1)}, u32[]{:S(2)}, u32[]{:S(2)}) async-start(bf16[16,2,16384]{2,1,0:T(2,128)(2,1)} %reshape.164), calls=%async_computation | async-start | bytes 2097152 | tf_op jit(solution)/shard_map/all_to_all | solution.py:95
  86.6 1.1 copy-start.6
  112.4 25.0 %copy-start.1 = (bf16[4,32,8192]{2,0,1:T(4,128)(2,1)S(1)}, bf16[4,32,8192]{2,0,1:T(4,128)(2,1)}, u32[]{:S(2)}) copy-start(bf16[4,32,8192]{2,0,1:T(4,128)(2,1)} %all-gather.3.cloned.1.call-done) | copy-start | bytes 6291460
  143.1 18.6 %copy-start.2 = (bf16[4,64,8,128,1]{3,2,1,0,4:T(8,128)(2,1)S(1)}, bf16[4,64,8,128,1]{3,2,1,0,4:T(8,128)(2,1)}, u32[]{:S(2)}) copy-start(bf16[4,64,8,128,1]{3,2,1,0,4:T(8,128)(2,1)} %bitcast_bitcast_fusion) | copy-start | bytes 1572868
  144.1 11.4 %all-to-all-start.1 = ((bf16[4,32,512]{2,0,1:T(4,128)(2,1)}), bf16[4,32,512]{2,0,1:T(4,128)(2,1)S(1)}, u32[]{:S(2)}, u32[]{:S(2)}) async-start(bf16[4,32,512]{2,0,1:T(4,128)(2,1)} %copy.84), calls=%async_computation.1 | async-start | bytes 262144 | tf_op jit(solution)/shard_map/all_to_all | solution.py:113
  164.9 7.0 %all-to-all-start.3 = ((f32[2,1,512]{2,1,0:T(1,128)}), f32[2,1,512]{2,1,0:T(1,128)S(1)}, u32[]{:S(2)}, u32[]{:S(2)}) async-start(f32[2,1,512]{2,1,0:T(1,128)} %reshape.166), calls=%async_computation.3 | async-start | bytes 8192 | tf_op jit(solution)/shard_map/all_to_all | solution.py:139
  171.9 7.0 %all-to-all-start.4 = ((f32[2,1,512]{2,1,0:T(1,128)}), f32[2,1,512]{2,1,0:T(1,128)S(1)}, u32[]{:S(2)}, u32[]{:S(2)}) async-start(f32[2,1,512]{2,1,0:T(1,128)} %reshape.168), calls=%async_computation.4 | async-start | bytes 8192 | tf_op jit(solution)/shard_map/all_to_all | solution.py:140
  178.9 10.1 %all-to-all-start.2 = ((f32[4,2,2,8,8,128]{5,4,0,3,2,1:T(8,128)}), f32[4,2,2,8,8,128]{5,4,0,3,2,1:T(8,128)S(1)}, u32[]{:S(2)}, u32[]{:S(2)}) async-start(f32[4,2,2,8,8,128]{5,4,0,3,2,1:T(8,128)} %bitcast.27), calls=%async_computation.2 | async-start | bytes 1048576 | tf_op jit(solution)/shard_map/all_to_all | solution.py:138
Sparse Core Ops, SparseCore 0:
  9.5 44.1 all-gather.2
where the time goes:
time: 198 us; the launch traced here: 197 us
  other arithmetic  47.7 us (24%)
  blocking collectives  45.5 us (23%)
  local copies, waits for them, and re-layouts  36 us (18%)
  starting transfers between devices  20.9 us (11%)
  waiting for transfers between devices  17.1 us (9%)
  between operations  15.1 us (8%)
  matrix products  15 us (8%)
    unnamed x1, other arithmetic  45.2 us
    unnamed x36, local copies, waits for them, and re-layouts  27.6 us
    all_gather x1, blocking collectives, body(): lax.all_gather(shrink.reshape(steps, slots, adapter_rank), 'ada', axis=1,...  19 us
    squeeze x1, blocking collectives, body(): row_adapter = group_ids[:, 0]  12.3 us
    all_to_all x1, starting transfers between devices, body(): lax.all_to_all(adapter_up, 'ada', split_axis=2, concat_axis=0, tiled=True)  7.42 us
    all_to_all x1, waiting for transfers between devices, body(): lax.all_to_all(query_columns, 'ada', split_axis=1, concat_axis=2, tiled=T...  6.79 us
    dot_general x1, matrix products, body(): jnp.dot(whole_inputs.reshape(steps * group, width), query_weight, preferr...  5.7 us
    all_to_all x1, waiting for transfers between devices, body(): lax.all_to_all(partial_numerator, 'dec', split_axis=1, concat_axis=1, til...  5.68 us
  transfers between devices with their start and end apart: 6, of which 4 were waited for; matrix products, arithmetic and copies ran while one was open for 40% of the time, Pallas kernels for 0%

commit v1 on v0

v1 whole, which is shorter than its diff:
```python
import functools
import math

import jax
import jax.numpy as jnp
from jax import lax
from jax.experimental import pallas as pl
from jax.experimental.pallas import tpu as pltpu
from jax.sharding import PartitionSpec as P

HD = 128
CAP = 4
LANES = 128
CHUNKS = 4
NEGATIVE = -1e30
MESH = pl.DeviceIdType.MESH
F32 = jnp.float32
BF16 = jnp.bfloat16


def nt_dot(a, b):
    return lax.dot_general(a, b, (((1,), (1,)), ((), ())), preferred_element_type=F32)


def iota(shape, axis):
    return lax.broadcasted_iota(jnp.int32, shape, axis)


def kernel(
    n,
    n_dec,
    x_ref,
    w_hbm,
    down_hbm,
    up_hbm,
    ids_ref,
    new_ref,
    pool_hbm,
    table_ref,
    len_ref,
    out_ref,
    *scratch,
):
    gathered = scratch[:CHUNKS]
    (
        w_ref, down_ref, up_ref, pages, base, shrink, d_send, d_recv, q_send, q_recv, keys, values,
        w_sem, down_sem, up_sem, pool_sem, pool_send, pool_recv,
        up_send, low_send, across_send, side_send, g_recv, ds_sem, dr_sem, qs_sem, qr_sem,
    ) = scratch[CHUNKS:]
    ada, dec = lax.axis_index("ada"), lax.axis_index("dec")
    steps, rows, width = x_ref.shape
    part = width // CHUNKS
    block = steps * rows
    total = n * block
    head_cols = w_ref.shape[1]
    slots = steps * CAP
    span = n // 4
    o, m, c = ada // 4, (ada // 2) % 2, ada % 2
    sibling = ada + 1 - 2 * c
    opposite = ada + 2 - 4 * m
    pool_local = pool_hbm.shape[0]

    def w_copy(k):
        where = pl.ds(k * part, part)
        return pltpu.make_async_copy(w_hbm.at[where], w_ref.at[where], w_sem.at[k])

    down_copy = pltpu.make_async_copy(down_hbm, down_ref, down_sem)
    up_copy = pltpu.make_async_copy(up_hbm, up_ref, up_sem)
    own_pages = pages.at[pl.ds(dec * pool_local, pool_local)]
    pool_copy = pltpu.make_async_copy(pool_hbm, own_pages, pool_sem)

    mine = jnp.concatenate([x_ref[t].astype(F32) for t in range(steps)], axis=0).astype(BF16)
    row_of = iota((block, LANES), 0) % rows
    id_block = jnp.zeros((block, LANES), F32)
    for r in range(rows):
        id_block = jnp.where(row_of == r, ids_ref[r].astype(F32), id_block)
    for k in range(CHUNKS):
        gathered[k][ada, :, 0:part] = mine[:, k * part : (k + 1) * part]
    gathered[0][ada, :, part : part + LANES] = id_block.astype(BF16)

    barrier = pltpu.get_barrier_semaphore()
    for d in range(1, n):
        pl.semaphore_signal(
            barrier, inc=1, device_id={"ada": lax.rem(ada + d, n)}, device_id_type=MESH
        )
    for d in range(1, n_dec):
        pl.semaphore_signal(
            barrier, inc=1, device_id={"dec": lax.rem(dec + d, n_dec)}, device_id_type=MESH
        )
    w_copy(0).start()
    down_copy.start()
    for k in range(1, CHUNKS):
        w_copy(k).start()
    up_copy.start()
    pool_copy.start()
    pl.semaphore_wait(barrier, n - 1 + n_dec - 1)

    def relay(k, source, send_sem, peer):
        return pltpu.make_async_remote_copy(
            src_ref=gathered[k].at[source],
            dst_ref=gathered[k].at[source],
            send_sem=send_sem,
            recv_sem=g_recv.at[k, source],
            device_id={"ada": peer},
            device_id_type=MESH,
        )

    def arrived(k, source):
        relay(k, source, side_send.at[k, 0], sibling).wait_recv()

    def upward(k, line):
        return relay(k, line * 4 + m * 2 + c, up_send.at[k, line], ada + 4)

    def downward(k, line):
        return relay(k, line * 4 + m * 2 + c, low_send.at[k, line], ada - 4)

    def across(k, line):
        return relay(k, line * 4 + m * 2 + c, across_send.at[k, line], opposite)

    def sideways(k, line, column):
        return relay(
            k, line * 4 + column * 2 + c, side_send.at[k, line * 2 + column], sibling
        )

    def send_own(k):
        across(k, o).start()

        @pl.when(o < span - 1)
        def _():
            upward(k, o).start()

        @pl.when(o > 0)
        def _():
            downward(k, o).start()

        sideways(k, o, m).start()

    def line_wave(k):
        for distance in range(1, span):
            below, above = o - distance, o + distance

            @pl.when(below >= 0)
            def _():
                arrived(k, below * 4 + m * 2 + c)
                across(k, below).start()

                @pl.when(o < span - 1)
                def _():
                    upward(k, below).start()

                sideways(k, below, m).start()

            @pl.when(above < span)
            def _():
                arrived(k, above * 4 + m * 2 + c)
                across(k, above).start()

                @pl.when(o > 0)
                def _():
                    downward(k, above).start()

                sideways(k, above, m).start()

    def across_wave(k):
        other = 1 - m
        arrived(k, o * 4 + other * 2 + c)
        sideways(k, o, other).start()
        for distance in range(1, span):
            below, above = o - distance, o + distance

            @pl.when(below >= 0)
            def _():
                arrived(k, below * 4 + other * 2 + c)
                sideways(k, below, other).start()

            @pl.when(above < span)
            def _():
                arrived(k, above * 4 + other * 2 + c)
                sideways(k, above, other).start()

    def side_wave(k):
        for line in range(span):
            for column in range(2):
                arrived(k, line * 4 + column * 2 + 1 - c)

    def chunk_rows(k):
        return gathered[k][:, :, 0:part].astype(F32).reshape(total, part).astype(BF16)

    def add_shrink(k, held):
        term = nt_dot(held, down_ref[:, k * part : (k + 1) * part])
        shrink[...] = term if k == 0 else shrink[...] + term

    def add_base(k, held):
        term = jnp.dot(held, w_ref[k * part : (k + 1) * part, :], preferred_element_type=F32)
        base[...] = term if k == 0 else base[...] + term

    def multiply(k):
        w_copy(k).wait()
        if k == 0:
            down_copy.wait()
        held = chunk_rows(k)
        add_shrink(k, held)
        if k < CHUNKS - 1:
            add_base(k, held)

    def pool_send_copy(d):
        return pltpu.make_async_remote_copy(
            src_ref=pool_hbm,
            dst_ref=own_pages,
            send_sem=pool_send.at[d],
            recv_sem=pool_recv.at[dec],
            device_id={"dec": lax.rem(dec + d, n_dec)},
            device_id_type=MESH,
        )

    def pool_arrived(owner):
        pltpu.make_async_remote_copy(
            src_ref=pool_hbm,
            dst_ref=pages.at[pl.ds(owner * pool_local, pool_local)],
            send_sem=pool_send.at[1],
            recv_sem=pool_recv.at[owner],
            device_id={"dec": lax.rem(dec + 1, n_dec)},
            device_id_type=MESH,
        ).wait_recv()

    send_own(0)
    for d in range(1, n_dec):
        pool_send_copy(d).start()
    send_own(1)
    for s in range(CHUNKS + 2):
        if s < CHUNKS:
            line_wave(s)
            if s + 2 < CHUNKS:
                send_own(s + 2)
        if 1 <= s <= CHUNKS:
            across_wave(s - 1)
        if s >= 2:
            side_wave(s - 2)
            multiply(s - 2)

    id_col = (
        gathered[0][:, :, part : part + LANES]
        .astype(F32)
        .reshape(total, LANES)[:, 0:1]
    )
    at_row, at_lane = iota((total, total), 0), iota((total, total), 1)
    id_row = jnp.sum(jnp.where(at_row == at_lane, id_col, 0.0), axis=0, keepdims=True)
    same = id_col == id_row
    row_rank = at_row // block * rows + at_row % rows
    lane_rank = at_lane // block * rows + at_lane % rows
    count_col = jnp.sum(
        jnp.where(same & (lane_rank < row_rank) & (at_lane % block < rows), 1.0, 0.0),
        axis=1,
        keepdims=True,
    )
    count_row = jnp.sum(
        jnp.where(same & (row_rank < lane_rank) & (at_row % block < rows), 1.0, 0.0),
        axis=0,
        keepdims=True,
    )
    slot, lane = iota((slots, total), 0), iota((slots, total), 1)
    pick = jnp.where(
        (slot // CAP == lane % block // rows)
        & (id_row == ada.astype(F32))
        & (count_row == (slot % CAP).astype(F32)),
        1.0,
        0.0,
    ).astype(BF16)
    row, place = iota((total, n * slots), 0), iota((total, n * slots), 1)
    spread = jnp.where(
        (row % block // rows == place % slots // CAP)
        & (id_col == (place // slots).astype(F32))
        & (count_col == (place % CAP).astype(F32)),
        1.0,
        0.0,
    ).astype(BF16)

    chosen = jnp.dot(pick, shrink[...].astype(BF16), preferred_element_type=F32).astype(BF16)
    up_copy.wait()

    def delta_of(target):
        columns = pl.ds(pl.multiple_of(target * head_cols, head_cols), head_cols)
        return jnp.dot(chosen, up_ref[:, columns], preferred_element_type=F32).astype(BF16)

    def d_copy(target):
        return pltpu.make_async_remote_copy(
            src_ref=d_send.at[target],
            dst_ref=d_recv.at[ada],
            send_sem=ds_sem.at[target],
            recv_sem=dr_sem.at[ada],
            device_id={"ada": target},
            device_id_type=MESH,
        )

    def d_arrived(source):
        pltpu.make_async_remote_copy(
            src_ref=d_send.at[source],
            dst_ref=d_recv.at[source],
            send_sem=ds_sem.at[source],
            recv_sem=dr_sem.at[source],
            device_id={"ada": source},
            device_id_type=MESH,
        ).wait_recv()

    order = sorted(range(1, n), key=lambda d: (abs(d - n // 2), d))
    targets = [lax.rem(ada + d, n) for d in order]
    sources = [lax.rem(ada + n - d, n) for d in order]
    for i, target in enumerate(targets):
        d_send[target] = delta_of(target)
        if i > 0:
            d_copy(targets[i - 1]).start()
    d_recv[ada] = delta_of(ada)
    d_copy(targets[-1]).start()

    add_base(CHUNKS - 1, chunk_rows(CHUNKS - 1))

    pool_copy.wait()
    for d in range(1, n_dec):
        pool_arrived(lax.rem(dec + d, n_dec))
    entries, page = table_ref.shape[1], pages.shape[2]
    cached = rows * entries * page
    for r in range(rows):
        for j in range(entries):
            held = pages[table_ref[r, j]]
            first = (r * entries + j) * page
            keys[first : first + page, :] = held[0]
            values[first : first + page, :] = held[1]
    fresh = [new_ref[u, r].astype(F32) for u in range(steps) for r in range(rows)]
    empty = jnp.zeros((keys.shape[0] - cached - block, keys.shape[1]), F32)
    keys[cached:, :] = jnp.concatenate([f[0:1] for f in fresh] + [empty], axis=0).astype(BF16)
    values[cached:, :] = jnp.concatenate([f[1:2] for f in fresh] + [empty], axis=0).astype(BF16)

    for source in sources:
        d_arrived(source)
    update = jnp.dot(
        spread, d_recv[...].reshape(n * slots, head_cols), preferred_element_type=F32
    )
    q_send[...] = (base[...] + update).reshape(n, block, head_cols).astype(BF16)
    q_recv[ada] = q_send[ada]

    def q_copy(target):
        return pltpu.make_async_remote_copy(
            src_ref=q_send.at[target],
            dst_ref=q_recv.at[ada],
            send_sem=qs_sem.at[target],
            recv_sem=qr_sem.at[ada],
            device_id={"ada": target},
            device_id_type=MESH,
        )

    def q_arrived(source):
        pltpu.make_async_remote_copy(
            src_ref=q_send.at[source],
            dst_ref=q_recv.at[source],
            send_sem=qs_sem.at[source],
            recv_sem=qr_sem.at[source],
            device_id={"ada": source},
            device_id_type=MESH,
        ).wait_recv()

    for target in targets:
        q_copy(target).start()

    kv_heads = keys.shape[1] // HD
    heads = width // HD
    group = heads // kv_heads
    count = keys.shape[0]
    query_at, key_at = iota((group * block, count), 0), iota((group * block, count), 1)
    query_step, query_row = query_at % block // rows, query_at % rows
    limit = jnp.zeros((group * block, count), jnp.int32)
    for r in range(rows):
        limit = jnp.where(query_row == r, len_ref[r], limit)
    in_cache = (
        (key_at < cached)
        & (key_at // (entries * page) == query_row)
        & (key_at % (entries * page) < limit)
    )
    late = key_at - cached
    in_new = (late >= 0) & (late % rows == query_row) & (late // rows <= query_step)
    allowed = in_cache | in_new
    scale = 1.0 / math.sqrt(HD)

    for source in sources:
        q_arrived(source)
    per_source = head_cols // HD
    for h in range(kv_heads):
        parts = []
        for g in range(group):
            head = h * group + g
            first = head % per_source * HD
            parts.append(q_recv[head // per_source, :, first : first + HD].astype(F32))
        query = jnp.concatenate(parts, axis=0).astype(BF16)
        lanes = slice(h * HD, (h + 1) * HD)
        scores = jnp.where(allowed, nt_dot(query, keys[:, lanes]) * scale, NEGATIVE)
        top = jnp.max(scores, axis=1, keepdims=True)
        weights = jnp.where(allowed, jnp.exp(scores - top), 0.0)
        denominator = jnp.sum(weights, axis=1, keepdims=True)
        high = weights.astype(BF16)
        low = (weights - high.astype(F32)).astype(BF16)
        both = jnp.dot(
            jnp.concatenate([high, low], axis=0), values[:, lanes], preferred_element_type=F32
        )
        attended = (both[: group * block] + both[group * block :]) / denominator
        for g in range(group):
            first = (h * group + g) * HD
            out_ref[:, first : first + HD] = attended[g * block : (g + 1) * block].astype(BF16)

    for k in range(CHUNKS):
        for line in range(span):
            across(k, line).wait_send()

            @pl.when((line <= o) & (o < span - 1))
            def _():
                upward(k, line).wait_send()

            @pl.when((line >= o) & (o > 0))
            def _():
                downward(k, line).wait_send()

            for column in range(2):
                sideways(k, line, column).wait_send()
    for d in range(1, n_dec):
        pool_send_copy(d).wait_send()
    for target in targets:
        d_copy(target).wait_send()
        q_copy(target).wait_send()


def body(
    inputs,
    query_weight,
    adapter_down,
    adapter_up,
    adapter_ids,
    new_cache,
    cache_pool,
    page_table,
    lengths,
):
    n, n_dec = lax.axis_size("ada"), lax.axis_size("dec")
    steps, rows, width = inputs.shape
    held, _, rank = adapter_down.shape
    assert held == 1 and n % 4 == 0
    head_cols = query_weight.shape[1]
    block, slots, span = steps * rows, steps * CAP, n // 4
    part = width // CHUNKS
    pool_local, _, page, kv_width = cache_pool.shape
    count = -(-(rows * page_table.shape[1] * page + block) // 16) * 16
    dma = pltpu.SemaphoreType.DMA
    vmem, smem, hbm = (
        pl.BlockSpec(memory_space=pltpu.VMEM),
        pl.BlockSpec(memory_space=pltpu.SMEM),
        pl.BlockSpec(memory_space=pl.ANY),
    )
    scratch = [
        pltpu.VMEM((n, block, part + (LANES if k == 0 else 0)), BF16) for k in range(CHUNKS)
    ] + [
        pltpu.VMEM((width, head_cols), BF16),
        pltpu.VMEM((rank, width), BF16),
        pltpu.VMEM((rank, width), BF16),
        pltpu.VMEM((n_dec * pool_local, 2, page, kv_width), BF16),
        pltpu.VMEM((n * block, head_cols), F32),
        pltpu.VMEM((n * block, rank), F32),
        pltpu.VMEM((n, slots, head_cols), BF16),
        pltpu.VMEM((n, slots, head_cols), BF16),
        pltpu.VMEM((n, block, head_cols), BF16),
        pltpu.VMEM((n, block, head_cols), BF16),
        pltpu.VMEM((count, kv_width), BF16),
        pltpu.VMEM((count, kv_width), BF16),
        dma((CHUNKS,)),
        dma,
        dma,
        dma,
        dma((n_dec,)),
        dma((n_dec,)),
        dma((CHUNKS, span)),
        dma((CHUNKS, span)),
        dma((CHUNKS, span)),
        dma((CHUNKS, 2 * span)),
        dma((CHUNKS, n)),
        dma((n,)),
        dma((n,)),
        dma((n,)),
        dma((n,)),
    ]
    out = pl.pallas_call(
        functools.partial(kernel, n, n_dec),
        out_shape=jax.ShapeDtypeStruct((block, width), BF16),
        in_specs=[vmem, hbm, hbm, hbm, smem, vmem, hbm, smem, smem],
        out_specs=vmem,
        scratch_shapes=scratch,
        compiler_params=pltpu.CompilerParams(
            collective_id=0, has_side_effects=True, vmem_limit_bytes=60 * 1024 * 1024
        ),
    )(
        inputs,
        query_weight,
        jnp.swapaxes(adapter_down[0], 0, 1),
        adapter_up[0],
        adapter_ids[:, 0],
        new_cache,
        cache_pool,
        page_table,
        lengths,
    )
    return out.reshape(steps, rows, width)


def solution(mesh):
    in_specs = (
        P(None, ("dec", "ada"), None),
        P(None, "ada"),
        P(("dec", "ada"), None, None),
        P(("dec", "ada"), None, None),
        P(("dec", "ada"), None),
        P(None, ("dec", "ada"), None, None),
        P(("dec", "ada"), None, None, None),
        P(("dec", "ada"), None),
        P(("dec", "ada")),
    )
    out_specs = P(None, ("dec", "ada"), None)
    return jax.shard_map(body, mesh=mesh, in_specs=in_specs, out_specs=out_specs, check_vma=False)
```

time: 198 us -> 51.2 us (0.26)
  Pallas kernels: 0 us -> 49.4 us
  other arithmetic: 47.7 us -> 0 us
  blocking collectives: 45.5 us -> 0 us
  local copies, waits for them, and re-layouts: 36 us -> 1.67 us
  starting transfers between devices: 20.9 us -> 0 us
  waiting for transfers between devices: 17.1 us -> 0 us
  between operations: 15.1 us -> 0.01 us
  matrix products: 15 us -> 0 us
    pallas_call x0 -> x1, Pallas kernels: none -> 49.4 us  [body(): pl.pallas_call(functools.partial(kernel, n, n_dec), out_shape=jax.ShapeDt...]
    unnamed x1 -> x0, other arithmetic: 45.2 us -> none
    all_gather x3 -> x0, blocking collectives: 28.9 us -> none  [the longest x1 19 us: body(): lax.all_gather(shrink.reshape(steps, slots, adapter_rank), 'ada', axis=1,...]
    unnamed x36 -> x0, local copies, waits for them, and re-layouts: 27.6 us -> none
    all_to_all x5 -> x0, starting transfers between devices: 20.9 us -> none  [the longest x1 7.42 us: body(): lax.all_to_all(adapter_up, 'ada', split_axis=2, concat_axis=0, tiled=True)]
    all_to_all x5 -> x0, waiting for transfers between devices: 17.1 us -> none  [the longest x1 6.79 us: body(): lax.all_to_all(query_columns, 'ada', split_axis=1, concat_axis=2, tiled=T...]
    dot_general x8 -> x0, matrix products: 15 us -> none  [the longest x1 5.7 us: body(): jnp.dot(whole_inputs.reshape(steps * group, width), query_weight, preferr...]
    squeeze x1 -> x0, blocking collectives: 12.3 us -> none  [body(): row_adapter = group_ids[:, 0]]
  transfers between devices with their start and end apart: 6 -> 0, of which waited for: 4 -> 0; matrix products, arithmetic and copies ran while one was open for 40% -> 0% of each run, Pallas kernels for 0% -> 0%
where the time goes in v1:
time: 51.2 us; the launch traced here: 51 us
  Pallas kernels  49.4 us (96%)
  local copies, waits for them, and re-layouts  1.67 us (3%)
    pallas_call x1, Pallas kernels, body(): pl.pallas_call(functools.partial(kernel, n, n_dec), out_shape=jax.ShapeDt...  49.4 us
    reshape x1, local copies, waits for them, and re-layouts, body(): return out.reshape(steps, rows, width)  1.67 us

profile of v1, /device:TPU:0, one launch (start us, length us, event | category | flops | bytes accessed | tf_op | source)
XLA Modules:
  0.0 51.0 jit_solution(10303909793476858655)
XLA Ops:
  0.0 49.4 %shard_map.91 = bf16[8,8192]{1,0:T(8,128)(2,1)} custom-call(bf16[4,2,8192]{2,1,0:T(2,128)(2,1)} %x_ref.1, bf16[8192,512]{1,0:T(8,128)(2,1)} %w_hbm.1, bf16[64,8192]{1,0:T(8,128)(2,1)} %bitcast.5, bf16[64,8192]{1,0:T(8,128)(2,1)} %bitcast.6, s32[2]{0:T(128)} %bitcast.7, bf16[4,2,2,1024]{3,2,1,0:T(2,128)(2,1)} %new_ref.1, bf16[8,2,16,1024]{3,2,1,0:T(8,128)(2,1)} %pool_hbm.1, ...), custom_call_target="tpu_custom_call" | custom-call | tf_op jit(solution)/shard_map/pallas_call | solution.py:486
  49.4 1.7 %reshape.3 = bf16[4,2,8192]{2,1,0:T(2,128)(2,1)} reshape(bf16[8,8192]{1,0:T(8,128)(2,1)} %shard_map.91) | data formatting | bytes 262144 | tf_op jit(solution)/shard_map/reshape | solution.py:506

commit v2 on v1

--- a/solution.py
+++ b/solution.py
@@ -11,7 +11,9 @@
 HD = 128
 CAP = 4
 LANES = 128
-CHUNKS = 4
+CHUNKS = 2
+AHEAD = 2
+REACH = 2
 NEGATIVE = -1e30
 MESH = pl.DeviceIdType.MESH
 F32 = jnp.float32
@@ -43,7 +45,7 @@
 ):
     gathered = scratch[:CHUNKS]
     (
-        w_ref, down_ref, up_ref, pages, base, shrink, d_send, d_recv, q_send, q_recv, keys, values,
+        w_ref, down_ref, up_ref, pages, base, shrink, d_send, d_recv, q_send, q_recv, keys, values, result,
         w_sem, down_sem, up_sem, pool_sem, pool_send, pool_recv,
         up_send, low_send, across_send, side_send, g_recv, ds_sem, dr_sem, qs_sem, qr_sem,
     ) = scratch[CHUNKS:]
@@ -79,10 +81,22 @@
     gathered[0][ada, :, part : part + LANES] = id_block.astype(BF16)
 
     barrier = pltpu.get_barrier_semaphore()
-    for d in range(1, n):
-        pl.semaphore_signal(
-            barrier, inc=1, device_id={"ada": lax.rem(ada + d, n)}, device_id_type=MESH
-        )
+
+    def greet(peer):
+        pl.semaphore_signal(barrier, inc=1, device_id={"ada": peer}, device_id_type=MESH)
+
+    greet(opposite)
+    greet(sibling)
+    for distance in range(1, min(REACH, span - 1) + 1):
+        for side in (1, -1):
+
+            @pl.when((o + side * distance >= 0) & (o + side * distance < span))
+            def _():
+                greet(ada + 4 * side * distance)
+
+    line_peers = 0
+    for distance in range(1, min(REACH, span - 1) + 1):
+        line_peers += (o >= distance).astype(jnp.int32) + (o + distance < span).astype(jnp.int32)
     for d in range(1, n_dec):
         pl.semaphore_signal(
             barrier, inc=1, device_id={"dec": lax.rem(dec + d, n_dec)}, device_id_type=MESH
@@ -93,7 +107,7 @@
         w_copy(k).start()
     up_copy.start()
     pool_copy.start()
-    pl.semaphore_wait(barrier, n - 1 + n_dec - 1)
+    pl.semaphore_wait(barrier, line_peers + 2 + n_dec - 1)
 
     def relay(k, source, send_sem, peer):
         return pltpu.make_async_remote_copy(
@@ -114,6 +128,12 @@
     def downward(k, line):
         return relay(k, line * 4 + m * 2 + c, low_send.at[k, line], ada - 4)
 
+    def far_up(k):
+        return relay(k, ada, up_send.at[k, span], ada + 8)
+
+    def far_down(k):
+        return relay(k, ada, low_send.at[k, span], ada - 8)
+
     def across(k, line):
         return relay(k, line * 4 + m * 2 + c, across_send.at[k, line], opposite)
 
@@ -133,45 +153,53 @@
         def _():
             downward(k, o).start()
 
+        @pl.when(o < span - 2)
+        def _():
+            far_up(k).start()
+
+        @pl.when(o > 1)
+        def _():
+            far_down(k).start()
+
         sideways(k, o, m).start()
 
-    def line_wave(k):
-        for distance in range(1, span):
-            below, above = o - distance, o + distance
-
-            @pl.when(below >= 0)
-            def _():
-                arrived(k, below * 4 + m * 2 + c)
-                across(k, below).start()
+    def line_event(k, distance):
+        below, above = o - distance, o + distance
+
+        @pl.when(below >= 0)
+        def _():
+            arrived(k, below * 4 + m * 2 + c)
+            across(k, below).start()
+            if distance >= REACH:
 
                 @pl.when(o < span - 1)
                 def _():
                     upward(k, below).start()
 
-                sideways(k, below, m).start()
-
-            @pl.when(above < span)
-            def _():
-                arrived(k, above * 4 + m * 2 + c)
-                across(k, above).start()
+            sideways(k, below, m).start()
+
+        @pl.when(above < span)
+        def _():
+            arrived(k, above * 4 + m * 2 + c)
+            across(k, above).start()
+            if distance >= REACH:
 
                 @pl.when(o > 0)
                 def _():
                     downward(k, above).start()
 
-                sideways(k, above, m).start()
-
-    def across_wave(k):
+            sideways(k, above, m).start()
+
+    def across_event(k, distance):
         other = 1 - m
-        arrived(k, o * 4 + other * 2 + c)
-        sideways(k, o, other).start()
-        for distance in range(1, span):
-            below, above = o - distance, o + distance
-
-            @pl.when(below >= 0)
-            def _():
-                arrived(k, below * 4 + other * 2 + c)
-                sideways(k, below, other).start()
+        below, above = o - distance, o + distance
+
+        @pl.when(below >= 0)
+        def _():
+            arrived(k, below * 4 + other * 2 + c)
+            sideways(k, below, other).start()
+
+        if distance:
 
             @pl.when(above < span)
             def _():
@@ -223,57 +251,93 @@
             device_id_type=MESH,
         ).wait_recv()
 
-    send_own(0)
-    for d in range(1, n_dec):
-        pool_send_copy(d).start()
-    send_own(1)
-    for s in range(CHUNKS + 2):
-        if s < CHUNKS:
-            line_wave(s)
-            if s + 2 < CHUNKS:
-                send_own(s + 2)
-        if 1 <= s <= CHUNKS:
-            across_wave(s - 1)
-        if s >= 2:
-            side_wave(s - 2)
-            multiply(s - 2)
-
-    id_col = (
-        gathered[0][:, :, part : part + LANES]
-        .astype(F32)
-        .reshape(total, LANES)[:, 0:1]
-    )
-    at_row, at_lane = iota((total, total), 0), iota((total, total), 1)
-    id_row = jnp.sum(jnp.where(at_row == at_lane, id_col, 0.0), axis=0, keepdims=True)
-    same = id_col == id_row
-    row_rank = at_row // block * rows + at_row % rows
-    lane_rank = at_lane // block * rows + at_lane % rows
-    count_col = jnp.sum(
-        jnp.where(same & (lane_rank < row_rank) & (at_lane % block < rows), 1.0, 0.0),
-        axis=1,
-        keepdims=True,
-    )
-    count_row = jnp.sum(
-        jnp.where(same & (row_rank < lane_rank) & (at_row % block < rows), 1.0, 0.0),
-        axis=0,
-        keepdims=True,
-    )
-    slot, lane = iota((slots, total), 0), iota((slots, total), 1)
-    pick = jnp.where(
-        (slot // CAP == lane % block // rows)
-        & (id_row == ada.astype(F32))
-        & (count_row == (slot % CAP).astype(F32)),
-        1.0,
-        0.0,
-    ).astype(BF16)
-    row, place = iota((total, n * slots), 0), iota((total, n * slots), 1)
-    spread = jnp.where(
-        (row % block // rows == place % slots // CAP)
-        & (id_col == (place // slots).astype(F32))
-        & (count_col == (place % CAP).astype(F32)),
-        1.0,
-        0.0,
-    ).astype(BF16)
+    def slot_masks():
+        id_col = (
+            gathered[0][:, :, part : part + LANES]
+            .astype(F32)
+            .reshape(total, LANES)[:, 0:1]
+        )
+        at_row, at_lane = iota((total, total), 0), iota((total, total), 1)
+        id_row = jnp.sum(jnp.where(at_row == at_lane, id_col, 0.0), axis=0, keepdims=True)
+        same = id_col == id_row
+        row_rank = at_row // block * rows + at_row % rows
+        lane_rank = at_lane // block * rows + at_lane % rows
+        count_col = jnp.sum(
+            jnp.where(same & (lane_rank < row_rank) & (at_lane % block < rows), 1.0, 0.0),
+            axis=1,
+            keepdims=True,
+        )
+        count_row = jnp.sum(
+            jnp.where(same & (row_rank < lane_rank) & (at_row % block < rows), 1.0, 0.0),
+            axis=0,
+            keepdims=True,
+        )
+        slot, lane = iota((slots, total), 0), iota((slots, total), 1)
+        pick = jnp.where(
+            (slot // CAP == lane % block // rows)
+            & (id_row == ada.astype(F32))
+            & (count_row == (slot % CAP).astype(F32)),
+            1.0,
+            0.0,
+        ).astype(BF16)
+        row, place = iota((total, n * slots), 0), iota((total, n * slots), 1)
+        spread = jnp.where(
+            (row % block // rows == place % slots // CAP)
+            & (id_col == (place // slots).astype(F32))
+            & (count_col == (place % CAP).astype(F32)),
+            1.0,
+            0.0,
+        ).astype(BF16)
+        return pick, spread
+
+    entries, page = table_ref.shape[1], pages.shape[2]
+    cached = rows * entries * page
+    kv_heads = keys.shape[1] // HD
+    heads = width // HD
+    group = heads // kv_heads
+    count = keys.shape[0]
+
+    def key_mask():
+        query_at, key_at = iota((group * block, count), 0), iota((group * block, count), 1)
+        query_step, query_row = query_at % block // rows, query_at % rows
+        limit = jnp.zeros((group * block, count), jnp.int32)
+        for r in range(rows):
+            limit = jnp.where(query_row == r, len_ref[r], limit)
+        in_cache = (
+            (key_at < cached)
+            & (key_at // (entries * page) == query_row)
+            & (key_at % (entries * page) < limit)
+        )
+        late = key_at - cached
+        in_new = (late >= 0) & (late % rows == query_row) & (late // rows <= query_step)
+        return in_cache | in_new
+
+    for k in range(min(AHEAD, CHUNKS)):
+        send_own(k)
+        if k == 0:
+            for d in range(1, n_dec):
+                pool_send_copy(d).start()
+    lag = max(0, span - 1 - REACH)
+    pick = spread = allowed = id_col = None
+    for tick in range(CHUNKS + lag + 2):
+        for distance in range(1, span):
+            k = tick - max(0, distance - REACH)
+            if 0 <= k < CHUNKS:
+                line_event(k, distance)
+        if tick + AHEAD < CHUNKS:
+            send_own(tick + AHEAD)
+        for distance in range(span):
+            k = tick - 1 - max(0, distance - REACH)
+            if 0 <= k < CHUNKS:
+                across_event(k, distance)
+        k = tick - lag - 2
+        if 0 <= k < CHUNKS:
+            side_wave(k)
+            multiply(k)
+            if k == 0:
+                pick, spread = slot_masks()
+            if k == min(1, CHUNKS - 1):
+                allowed = key_mask()
 
     chosen = jnp.dot(pick, shrink[...].astype(BF16), preferred_element_type=F32).astype(BF16)
     up_copy.wait()
@@ -317,8 +381,6 @@
     pool_copy.wait()
     for d in range(1, n_dec):
         pool_arrived(lax.rem(dec + d, n_dec))
-    entries, page = table_ref.shape[1], pages.shape[2]
-    cached = rows * entries * page
     for r in range(rows):
         for j in range(entries):
             held = pages[table_ref[r, j]]
@@ -361,23 +423,6 @@
     for target in targets:
         q_copy(target).start()
 
-    kv_heads = keys.shape[1] // HD
-    heads = width // HD
-    group = heads // kv_heads
-    count = keys.shape[0]
-    query_at, key_at = iota((group * block, count), 0), iota((group * block, count), 1)
-    query_step, query_row = query_at % block // rows, query_at % rows
-    limit = jnp.zeros((group * block, count), jnp.int32)
-    for r in range(rows):
-        limit = jnp.where(query_row == r, len_ref[r], limit)
-    in_cache = (
-        (key_at < cached)
-        & (key_at // (entries * page) == query_row)
-        & (key_at % (entries * page) < limit)
-    )
-    late = key_at - cached
-    in_new = (late >= 0) & (late % rows == query_row) & (late // rows <= query_step)
-    allowed = in_cache | in_new
     scale = 1.0 / math.sqrt(HD)
 
     for source in sources:
@@ -403,17 +448,29 @@
         attended = (both[: group * block] + both[group * block :]) / denominator
         for g in range(group):
             first = (h * group + g) * HD
-            out_ref[:, first : first + HD] = attended[g * block : (g + 1) * block].astype(BF16)
+            result[:, first : first + HD] = attended[g * block : (g + 1) * block]
+
+    for t in range(steps):
+        out_ref[t] = result[t * rows : (t + 1) * rows, :].astype(BF16)
 
     for k in range(CHUNKS):
+
+        @pl.when(o < span - 2)
+        def _():
+            far_up(k).wait_send()
+
+        @pl.when(o > 1)
+        def _():
+            far_down(k).wait_send()
+
         for line in range(span):
             across(k, line).wait_send()
 
-            @pl.when((line <= o) & (o < span - 1))
+            @pl.when(((line == o) | (line <= o - REACH)) & (o < span - 1))
             def _():
                 upward(k, line).wait_send()
 
-            @pl.when((line >= o) & (o > 0))
+            @pl.when(((line == o) | (line >= o + REACH)) & (o > 0))
             def _():
                 downward(k, line).wait_send()
 
@@ -467,14 +524,15 @@
         pltpu.VMEM((n, block, head_cols), BF16),
         pltpu.VMEM((count, kv_width), BF16),
         pltpu.VMEM((count, kv_width), BF16),
+        pltpu.VMEM((block, width), F32),
         dma((CHUNKS,)),
         dma,
         dma,
         dma,
         dma((n_dec,)),
         dma((n_dec,)),
-        dma((CHUNKS, span)),
-        dma((CHUNKS, span)),
+        dma((CHUNKS, span + 1)),
+        dma((CHUNKS, span + 1)),
         dma((CHUNKS, span)),
         dma((CHUNKS, 2 * span)),
         dma((CHUNKS, n)),
@@ -483,9 +541,9 @@
         dma((n,)),
         dma((n,)),
     ]
-    out = pl.pallas_call(
+    return pl.pallas_call(
         functools.partial(kernel, n, n_dec),
-        out_shape=jax.ShapeDtypeStruct((block, width), BF16),
+        out_shape=jax.ShapeDtypeStruct((steps, rows, width), BF16),
         in_specs=[vmem, hbm, hbm, hbm, smem, vmem, hbm, smem, smem],
         out_specs=vmem,
         scratch_shapes=scratch,
@@ -503,7 +561,6 @@
         page_table,
         lengths,
     )
-    return out.reshape(steps, rows, width)
 
 
 def solution(mesh):

time: 51.2 us -> 43.6 us (0.85)
  Pallas kernels: 49.4 us -> 41.8 us
    pallas_call x1, Pallas kernels: 49.4 us -> 41.8 us  [body(): pl.pallas_call(functools.partial(kernel, n, n_dec), out_shape=jax.ShapeDt...]
    reshape x1 -> x0, local copies, waits for them, and re-layouts: 1.67 us -> none  [body(): return out.reshape(steps, rows, width)]
    unnamed x0 -> x1, local copies, waits for them, and re-layouts: none -> 1.65 us
where the time goes in v2:
time: 43.6 us; the launch traced here: 43.5 us
  Pallas kernels  41.8 us (96%)
  local copies, waits for them, and re-layouts  1.65 us (4%)
    pallas_call x1, Pallas kernels, body(): pl.pallas_call(functools.partial(kernel, n, n_dec), out_shape=jax.ShapeDt...  41.8 us
    unnamed x1, local copies, waits for them, and re-layouts  1.65 us

profile of v2, /device:TPU:0, one launch (start us, length us, event | category | flops | bytes accessed | tf_op | source)
XLA Modules:
  0.0 43.5 jit_solution(4879216461907193556)
XLA Ops:
  0.0 41.8 %shard_map.91 = bf16[4,2,8192]{2,1,0:T(2,128)(2,1)} custom-call(bf16[4,2,8192]{2,1,0:T(2,128)(2,1)} %x_ref.1, bf16[8192,512]{1,0:T(8,128)(2,1)} %w_hbm.1, bf16[64,8192]{1,0:T(8,128)(2,1)} %bitcast.5, bf16[64,8192]{1,0:T(8,128)(2,1)} %bitcast.6, s32[2]{0:T(128)} %bitcast.7, bf16[4,2,2,1024]{3,2,1,0:T(2,128)(2,1)} %new_ref.1, ...), custom_call_target="tpu_custom_call" | custom-call | tf_op jit(solution)/shard_map/pallas_call | solution.py:544
  41.8 1.7 %copy.11 = bf16[4,2,8192]{2,1,0:T(2,128)(2,1)} copy(bf16[4,2,8192]{2,1,0:T(2,128)(2,1)} %shard_map.91) | data formatting | bytes 262144

commit v3 on v2

--- a/solution.py
+++ b/solution.py
@@ -12,6 +12,7 @@
 CAP = 4
 LANES = 128
 CHUNKS = 2
+EDGES = (0, 10, 16)
 AHEAD = 2
 REACH = 2
 NEGATIVE = -1e30
@@ -51,7 +52,9 @@
     ) = scratch[CHUNKS:]
     ada, dec = lax.axis_index("ada"), lax.axis_index("dec")
     steps, rows, width = x_ref.shape
-    part = width // CHUNKS
+    edges = [width // EDGES[-1] * e for e in EDGES]
+    sizes = [b - a for a, b in zip(edges[:-1], edges[1:])]
+    part = sizes[0]
     block = steps * rows
     total = n * block
     head_cols = w_ref.shape[1]
@@ -63,7 +66,7 @@
     pool_local = pool_hbm.shape[0]
 
     def w_copy(k):
-        where = pl.ds(k * part, part)
+        where = pl.ds(edges[k], sizes[k])
         return pltpu.make_async_copy(w_hbm.at[where], w_ref.at[where], w_sem.at[k])
 
     down_copy = pltpu.make_async_copy(down_hbm, down_ref, down_sem)
@@ -77,7 +80,7 @@
     for r in range(rows):
         id_block = jnp.where(row_of == r, ids_ref[r].astype(F32), id_block)
     for k in range(CHUNKS):
-        gathered[k][ada, :, 0:part] = mine[:, k * part : (k + 1) * part]
+        gathered[k][ada, :, 0 : sizes[k]] = mine[:, edges[k] : edges[k + 1]]
     gathered[0][ada, :, part : part + LANES] = id_block.astype(BF16)
 
     barrier = pltpu.get_barrier_semaphore()
@@ -212,14 +215,14 @@
                 arrived(k, line * 4 + column * 2 + 1 - c)
 
     def chunk_rows(k):
-        return gathered[k][:, :, 0:part].astype(F32).reshape(total, part).astype(BF16)
+        return gathered[k][:, :, 0 : sizes[k]].astype(F32).reshape(total, sizes[k]).astype(BF16)
 
     def add_shrink(k, held):
-        term = nt_dot(held, down_ref[:, k * part : (k + 1) * part])
+        term = nt_dot(held, down_ref[:, edges[k] : edges[k + 1]])
         shrink[...] = term if k == 0 else shrink[...] + term
 
     def add_base(k, held):
-        term = jnp.dot(held, w_ref[k * part : (k + 1) * part, :], preferred_element_type=F32)
+        term = jnp.dot(held, w_ref[edges[k] : edges[k + 1], :], preferred_element_type=F32)
         base[...] = term if k == 0 else base[...] + term
 
     def multiply(k):
@@ -500,7 +503,9 @@
     assert held == 1 and n % 4 == 0
     head_cols = query_weight.shape[1]
     block, slots, span = steps * rows, steps * CAP, n // 4
-    part = width // CHUNKS
+    edges = [width // EDGES[-1] * e for e in EDGES]
+    sizes = [b - a for a, b in zip(edges[:-1], edges[1:])]
+    part = sizes[0]
     pool_local, _, page, kv_width = cache_pool.shape
     count = -(-(rows * page_table.shape[1] * page + block) // 16) * 16
     dma = pltpu.SemaphoreType.DMA
@@ -510,7 +515,7 @@
         pl.BlockSpec(memory_space=pl.ANY),
     )
     scratch = [
-        pltpu.VMEM((n, block, part + (LANES if k == 0 else 0)), BF16) for k in range(CHUNKS)
+        pltpu.VMEM((n, block, sizes[k] + (LANES if k == 0 else 0)), BF16) for k in range(CHUNKS)
     ] + [
         pltpu.VMEM((width, head_cols), BF16),
         pltpu.VMEM((rank, width), BF16),

time: 43.6 us -> 43.8 us (level)
  no operation moved by 1% of the time
where the time goes in v3:
time: 43.8 us; the launch traced here: 43.6 us
  Pallas kernels  42 us (96%)
  local copies, waits for them, and re-layouts  1.65 us (4%)
    pallas_call x1, Pallas kernels, body(): pl.pallas_call(functools.partial(kernel, n, n_dec), out_shape=jax.ShapeDt...  42 us
    unnamed x1, local copies, waits for them, and re-layouts  1.65 us

profile of v3, /device:TPU:0, one launch (start us, length us, event | category | flops | bytes accessed | tf_op | source)
XLA Modules:
  0.0 43.6 jit_solution(6643306121816486952)
XLA Ops:
  0.0 42.0 %shard_map.91 = bf16[4,2,8192]{2,1,0:T(2,128)(2,1)} custom-call(bf16[4,2,8192]{2,1,0:T(2,128)(2,1)} %x_ref.1, bf16[8192,512]{1,0:T(8,128)(2,1)} %w_hbm.1, bf16[64,8192]{1,0:T(8,128)(2,1)} %bitcast.5, bf16[64,8192]{1,0:T(8,128)(2,1)} %bitcast.6, s32[2]{0:T(128)} %bitcast.7, bf16[4,2,2,1024]{3,2,1,0:T(2,128)(2,1)} %new_ref.1, ...), custom_call_target="tpu_custom_call" | custom-call | tf_op jit(solution)/shard_map/pallas_call | solution.py:549
  42.0 1.7 %copy.11 = bf16[4,2,8192]{2,1,0:T(2,128)(2,1)} copy(bf16[4,2,8192]{2,1,0:T(2,128)(2,1)} %shard_map.91) | data formatting | bytes 262144
